TPU v7x, 128 devices: a whole 4x4x4 slice. The times are simulated.
128 devices in a mesh: slab: 16 (over z, x), pencil: 8 (over y, core).
Axes of the slice: x: 4, y: 4, z: 4, core: 2. Of those that a mesh axis runs over, the one named last changes fastest.
Arguments:
- a_blocks: float32 [256, 64, 20480], P('slab', 'pencil'), may hold values from -1 to 8, as said below
- col_codes: int32 [256, 64, 5], P('slab', 'pencil'), may hold values from 0 to 8, as said below
- agg_of: int32 [256, 64], P('slab', 'pencil'), may hold values from 0 to 2047, as said below
- test_vectors: float32 [256, 64, 2048], P('slab', 'pencil'), may hold values from -36 to 36
Outputs:
- relaxed: float32 [256, 64, 2048], P('slab', 'pencil')
- tiles: float32 [256, 64, 512], P('slab', 'pencil')
- products: float32 [256, 64, 2560], P('slab', 'pencil')
Inputs may be any that keep to these rules, and one draw needn't show every extreme that they name: `col_codes`: slot 0 of every block row is code 4, the block row itself; slots 1 to 4 hold different codes among the other eight of the 3 x 3 neighbourhood. `agg_of`: aggregate g is owned by device g // 16, devices numbered slab-major. On each device the block rows, in row-major order, form 64 groups of 2 consecutive block rows; all block rows of a group belong to aggregates of one owner, and the groups of one device go to different owners. Some owners receive a group from every device. `a_blocks`: the diagonal entries of every slot-0 block lie in [1.99, 8].
All inputs are finite; a program needn't handle non-finite values.
Results may differ from a plain program's by a relative error of at most 0.0003.
Values sent between devices are 32-bit elements; how exact they have to be, the bound alone decides.
A program may use at most 320 MiB of HBM per device.

v0:
```python
import math
import jax
import jax.numpy as jnp
from jax import lax
from jax.sharding import PartitionSpec as P

BLK = 64
NV = 32
NC = 8
KS = 5
ITERS = 2
OMEGA = 2.0 / 3.0
FULL_PRECISION = lax.Precision.HIGHEST


def with_halo(cells, sides, width):
    for axis, dim in sides:
        count = lax.axis_size(axis)
        ends = count - 1
        head = lax.slice_in_dim(cells, 0, width, axis=dim)
        tail = lax.slice_in_dim(cells, cells.shape[dim] - width, cells.shape[dim], axis=dim)
        cells = jnp.concatenate(
            [
                lax.ppermute(tail, axis, [(i, (i + 1) % count) for i in range(ends)]),
                cells,
                lax.ppermute(head, axis, [((i + 1) % count, i) for i in range(ends)]),
            ],
            axis=dim,
        )
    return cells


def coarse_modes(cells, coarse):
    centre = jnp.arange(cells, dtype=jnp.float32) + 0.5
    order = jnp.arange(coarse, dtype=jnp.float32)
    return jnp.cos(math.pi * centre[:, None] * order[None, :] / cells)


def solve_maps(coarse):
    gram = jnp.einsum("gkv,glv->gkl", coarse, coarse, precision=FULL_PRECISION)
    trace_sum = jnp.trace(gram, axis1=1, axis2=2)
    ridge = 0.1 * trace_sum / NC + 1e-06
    gram = gram + ridge[:, None, None] * jnp.eye(NC, dtype=jnp.float32)[None]
    lower = jnp.linalg.cholesky(gram)
    half_solved = jax.scipy.linalg.solve_triangular(lower, coarse, lower=True)
    solved = jax.scipy.linalg.solve_triangular(lower, half_solved, lower=True, trans=1)
    return jnp.swapaxes(solved, 1, 2)


def slot_index(col_codes):
    height, across_devices = (col_codes.shape[0], col_codes.shape[1])
    row_pos = jnp.arange(height, dtype=jnp.int32)[:, None, None] + col_codes // 3
    col_pos = jnp.arange(across_devices, dtype=jnp.int32)[None, :, None] + col_codes % 3
    return (row_pos * (across_devices + 2) + col_pos).reshape(-1)


def pick_rows(padded, flat_index, height, across_devices):
    features = padded.shape[2]
    flat = padded.reshape(padded.shape[0] * padded.shape[1], features)
    picked = jnp.take(flat, flat_index, axis=0)
    return picked.reshape(height, across_devices, KS, features)


def fit_slots(slot_coefficient, slot_ids, per_owner):
    members = (slot_ids[None, :] == jnp.arange(per_owner, dtype=jnp.int32)[:, None]).astype(
        jnp.float32
    )
    counts = jnp.sum(members, axis=1)
    summed = jnp.dot(
        members,
        slot_coefficient.reshape(slot_coefficient.shape[0], NC * NV),
        precision=FULL_PRECISION,
    )
    coarse = summed.reshape(per_owner, NC, NV) / jnp.maximum(counts, 1.0)[:, None, None]
    maps = solve_maps(coarse)
    return jnp.dot(members.T, maps.reshape(per_owner, NV * NC), precision=FULL_PRECISION)


def pack_slots(chosen_f, payload, group_list, capacity):
    flat = payload.reshape(group_list, capacity * payload.shape[1])
    packed = jnp.dot(chosen_f, flat, precision=FULL_PRECISION)
    return packed.reshape(chosen_f.shape[0], capacity, payload.shape[1])


def unpack_slots(chosen_f, received, block_rows):
    flat = received.reshape(received.shape[0], received.shape[1] * received.shape[2])
    return jnp.dot(chosen_f.T, flat, precision=FULL_PRECISION).reshape(
        block_rows, received.shape[2]
    )


def send_owner(payload, slot_ids):
    arrived, arrived_ids = (
        lax.all_to_all(payload, ("slab", "pencil"), split_axis=0, concat_axis=0, tiled=True),
        lax.all_to_all(slot_ids, ("slab", "pencil"), split_axis=0, concat_axis=0, tiled=True),
    )
    return (arrived, arrived_ids)


def send_back(payload):
    returned = lax.all_to_all(payload, ("slab", "pencil"), split_axis=0, concat_axis=0, tiled=True)
    return returned


def shards(a_blocks, col_codes, agg_of, test_vectors):
    height, across_devices = (agg_of.shape[0], agg_of.shape[1])
    n_slab = lax.axis_size("slab")
    n_pencil = lax.axis_size("pencil")
    devices = n_slab * n_pencil
    blocks = a_blocks.reshape(height, across_devices, KS, BLK, BLK)
    diagonal = jnp.diagonal(blocks[:, :, 0], axis1=-2, axis2=-1)
    block_wide = jnp.transpose(blocks, (0, 1, 3, 2, 4)).reshape(
        height, across_devices, BLK, KS * BLK
    )
    flat_index = slot_index(col_codes)
    candidate_vectors = test_vectors.reshape(height, across_devices, BLK, NV)
    for sweep in range(ITERS):
        padded = with_halo(
            candidate_vectors.reshape(height, across_devices, BLK * NV),
            (("slab", 0), ("pencil", 1)),
            1,
        )
        picked = pick_rows(padded, flat_index, height, across_devices).reshape(
            height, across_devices, KS * BLK, NV
        )
        image = jnp.einsum("ijor,ijrw->ijow", block_wide, picked, precision=FULL_PRECISION)
        candidate_vectors = candidate_vectors - OMEGA * image / diagonal[:, :, :, None]
    squares = jnp.sum(candidate_vectors * candidate_vectors, axis=(0, 1, 2))
    totals = lax.psum(squares, ("slab", "pencil"))
    scale = jnp.sqrt(totals / (height * across_devices * BLK * devices) + 1e-06)
    relaxed = candidate_vectors / scale
    block_rows = height * across_devices
    capacity = 2 * block_rows // devices
    group_list = devices // 2
    per_owner = block_rows // 8
    near_null_modes = coarse_modes(BLK, NC)
    row_vectors = relaxed.reshape(block_rows, BLK, NV)
    group_agg = agg_of.reshape(group_list, capacity)
    group_owner = group_agg[:, 0] // per_owner
    chosen = group_owner[None, :] == jnp.arange(devices, dtype=jnp.int32)[:, None]
    chosen_f = chosen.astype(jnp.float32)
    slot_ids = (
        jnp.sum(jnp.where(chosen[:, :, None], group_agg[None] % per_owner + 1, 0), axis=1) - 1
    )
    slot_count = devices * capacity
    outgoing = pack_slots(chosen_f, row_vectors.reshape(block_rows, BLK * NV), group_list, capacity)
    arrived, arrived_ids = send_owner(outgoing, slot_ids)
    slot_vector_rows = arrived.reshape(slot_count, BLK, NV)
    slot_coefficient = jnp.einsum(
        "wd,xwf->xdf", near_null_modes, slot_vector_rows, precision=FULL_PRECISION
    )
    slot_maps = fit_slots(slot_coefficient, arrived_ids.reshape(slot_count), per_owner)
    slot_tiles = jnp.einsum(
        "scv,svk->sck",
        slot_vector_rows,
        slot_maps.reshape(slot_count, NV, NC),
        precision=FULL_PRECISION,
    )
    returned = send_back(slot_tiles.reshape(devices, capacity, BLK * NC))
    tile_rows = unpack_slots(chosen_f, returned, block_rows).reshape(block_rows, BLK, NC)
    tile_grid = tile_rows.reshape(height, across_devices, BLK * NC)
    padded_tiles = with_halo(tile_grid, (("slab", 0), ("pencil", 1)), 1)
    picked_tiles = pick_rows(padded_tiles, flat_index, height, across_devices).reshape(
        height, across_devices, KS, BLK, NC
    )
    products = jnp.einsum("ijkoc,ijkcw->ijkow", blocks, picked_tiles, precision=FULL_PRECISION)
    return (
        relaxed.reshape(height, across_devices, BLK * NV),
        tile_grid,
        products.reshape(height, across_devices, KS * BLK * NC),
    )


def solution(mesh):
    in_specs = (
        P("slab", "pencil", None),
        P("slab", "pencil", None),
        P("slab", "pencil"),
        P("slab", "pencil", None),
    )
    out_specs = (P("slab", "pencil", None), P("slab", "pencil", None), P("slab", "pencil", None))
    return jax.shard_map(shards, mesh=mesh, in_specs=in_specs, out_specs=out_specs, check_vma=False)
```

profile of v0, /device:TPU:7, one launch (start us, length us, event | category | flops | bytes accessed | tf_op | source)
XLA Modules:
  0.0 639.7 jit_solution(15918062208513373529)
XLA Ops:
  1.6 2.5 collective-permute-start.1
  4.1 4.9 collective-permute-start
  11.9 38.9 %copy.177 = f32[16,8,20480]{0,1,2:T(8,128)} copy(f32[16,8,20480]{2,1,0:T(8,128)} %param.6) | data formatting | bytes 20971520 | tf_op args[0]
  50.9 11.6 %slice_bitcast_fusion = f32[16,8,64,64]{0,1,3,2:T(8,128)} fusion(f32[16,8,5,64,64]{0,1,4,3,2:T(8,128)} %bitcast), kind=kLoop, calls=%fused_computation.6 | loop fusion | bytes 4194304 | tf_op jit(solution)/shard_map/squeeze | solution.py:111
  63.2 4.3 collective-permute-start.2
  69.5 2.7 reshape.237
  72.2 3.8 copy.182
  76.0 6.4 %gather_fusion = f32[64,16,8]{1,2,0:T(8,128)S(1)} fusion(f32[16,8,64,64]{0,1,3,2:T(8,128)} %slice_bitcast_fusion, s32[64]{0:T(128)S(1)} %or_bitcast_fusion), kind=kCustom, calls=%fused_computation.2 | custom fusion | bytes 66048 | tf_op jit(solution)/shard_map/jit(diagonal)/gather | solution.py:111
  82.6 63.1 %copy.178 = f32[16,8,64,5,64]{2,4,3,1,0:T(8,128)} copy(f32[16,8,64,5,64]{0,1,4,2,3:T(8,128)} %bitcast.1) | data formatting | bytes 20971520 | tf_op jit(solution)/shard_map/transpose | solution.py:112
  146.0 2.3 copy.176
  150.0 4.6 gather_fusion.2
  154.6 5.2 broadcast_select_fusion.1
  159.8 13.7 %reshape_reshape.7 = f32[16,8,320,32]{3,2,1,0:T(8,128)} reshape(f32[640,2048]{1,0:T(8,128)} %broadcast_select_fusion.1) | data formatting | bytes 10485760 | tf_op jit(solution)/shard_map/reshape;reshape | solution.py:123
  173.5 37.9 %bitcast_subtract_fusion.1 = f32[16,8,64,32]{2,3,1,0:T(8,128)S(1)} fusion(f32[16,8,64,32]{2,3,1,0:T(8,128)} %copy.182, f32[16,8,320,32]{3,2,1,0:T(8,128)} %reshape_reshape.7, f32[16,8,64,320]{2,3,1,0:T(8,128)} %bitcast.82, f32[16,8,64]{2,1,0:T(8,128)S(1)} %copy.181), kind=kOutput, calls=%fused_computation.13 | convolution fusion | flops 1007419392 | bytes 17858560 | tf_op jit(solution)/shard_map/ijor,ijrw->ijow/dot_general | solution.py:126
  213.7 2.8 copy.184
  216.8 3.4 collective-permute-start.5
  220.2 3.6 reshape.242
  224.2 4.7 collective-permute-start.6
  231.6 10.5 %all-to-all-start.1 = ((s32[128,1,2]{2,1,0:T(1,128)}), s32[128,1,2]{2,1,0:T(1,128)S(1)}, u32[]{:S(2)}, u32[]{:S(2)}) async-start(s32[128,1,2]{2,1,0:T(1,128)} %copy.196), calls=%async_computation.1 | async-start | bytes 131072 | tf_op jit(solution)/shard_map/all_to_all | solution.py:95
  245.7 4.6 gather_fusion.3
  250.2 5.2 broadcast_select_fusion
  255.5 13.8 %reshape_reshape.8 = f32[16,8,320,32]{3,2,1,0:T(8,128)} reshape(f32[640,2048]{1,0:T(8,128)} %broadcast_select_fusion) | data formatting | bytes 10485760 | tf_op jit(solution)/shard_map/reshape;reshape | solution.py:123
  269.3 38.3 %multiply_reduce_fusion = (f32[32]{0:T(128)S(1)}, f32[16,8,64,32]{2,3,1,0:T(8,128)}) fusion(f32[16,8,64,32]{2,3,1,0:T(8,128)S(1)} %copy-done.1, f32[16,8,64]{2,1,0:T(8,128)S(1)} %copy.181, f32[16,8,320,32]{3,2,1,0:T(8,128)} %reshape_reshape.8, f32[16,8,64,320]{2,3,1,0:T(8,128)} %bitcast.83), kind=kOutput, calls=%fused_computation.14 | convolution fusion | flops 1007943680 | bytes 17858688 | tf_op jit(solution)/shard_map/ijor,ijrw->ijow/dot_general | solution.py:126
  307.6 65.2 %psum.7 = f32[32]{0:T(128)S(1)} all-reduce(f32[32]{0:T(128)S(1)} %get-tuple-element.33), channel_id=1, replica_groups=mesh['slab'=16,'pencil'=8] {'slab','pencil'}, use_global_device_ids=true, to_apply=%region_1.3 | all-reduce | flops 32 | bytes 256 | tf_op jit(solution)/shard_map/psum | solution.py:129
  374.8 2.8 copy.188
  377.6 3.5 reshape_reshape_reshape.6
  382.3 2.9 copy.192
  385.2 7.3 %all-to-all-start = ((f32[128,2,2048]{2,1,0:T(2,128)}), f32[128,2,2048]{2,1,0:T(2,128)S(1)}, u32[]{:S(2)}, u32[]{:S(2)}) async-start(f32[128,2,2048]{2,1,0:T(2,128)} %copy.192), calls=%async_computation | async-start | bytes 4194304 | tf_op jit(solution)/shard_map/all_to_all | solution.py:94
  394.1 26.8 %all-to-all-done = f32[128,2,2048]{2,1,0:T(2,128)S(1)} async-done(((f32[128,2,2048]{2,1,0:T(2,128)}), f32[128,2,2048]{2,1,0:T(2,128)S(1)}, u32[]{:S(2)}, u32[]{:S(2)}) %all-to-all-start) | async-done | bytes 2097184 | tf_op jit(solution)/shard_map/all_to_all | solution.py:94
  421.0 5.3 reshape.246
  426.3 7.0 %copy.197 = f32[256,64,32]{0,1,2:T(8,128)S(1)} copy(f32[256,64,32]{2,1,0:T(8,128)} %reshape.246) | data formatting | bytes 4194304 | tf_op jit(solution)/shard_map/reshape | solution.py:148
  435.6 11.7 %custom-call.11 = f32[16,8,8]{2,1,0:T(8,128)S(1)} custom-call(f32[16,8,8]{2,1,0:T(8,128)S(1)} %fusion.18), custom_call_target="Cholesky" | custom-call | tf_op jit(solution)/shard_map/jit(cholesky)/cholesky | solution.py:44
  447.6 10.0 %custom-call.12 = f32[16,1,8,8]{2,3,1,0:T(8,128)S(1)} custom-call(f32[16,1,8,8]{3,2,1,0:T(8,128)S(1)} %select_bitcast_fusion), custom_call_target="InvertDiagBlocksLowerTriangular" | custom-call | tf_op jit(solution)/shard_map/jit(_solve_triangular)/vmap()/triangular_solve | solution.py:46
  459.0 11.2 %fusion.56 = f32[256,64,8]{2,1,0:T(8,128)} fusion(f32[256,64,32]{2,1,0:T(8,128)} %reshape.246, f32[256,32,8]{1,2,0:T(8,128)S(1)} %copy.209), kind=kOutput, calls=%fused_computation.114 | convolution fusion | flops 50331648 | bytes 2883584 | tf_op jit(solution)/shard_map/scv,svk->sck/dot_general | solution.py:153
  470.2 7.4 %reshape.249 = f32[128,2,512]{2,1,0:T(2,128)} reshape(f32[256,64,8]{2,1,0:T(8,128)} %fusion.56) | data formatting | bytes 1048576 | tf_op jit(solution)/shard_map/reshape | solution.py:159
  477.6 6.3 all-to-all-start.2
  484.1 11.8 %all-to-all-done.2 = f32[128,2,512]{2,1,0:T(2,128)S(1)} async-done(((f32[128,2,512]{2,1,0:T(2,128)}), f32[128,2,512]{2,1,0:T(2,128)S(1)}, u32[]{:S(2)}, u32[]{:S(2)}) %all-to-all-start.2) | async-done | bytes 524320 | tf_op jit(solution)/shard_map/all_to_all | solution.py:101
  496.3 3.8 collective-permute-start.8
  502.2 4.6 collective-permute-done.9
  506.8 3.1 collective-permute-start.10
  509.9 2.7 collective-permute-start.11
  512.7 55.6 %copy.214 = f32[16,8,5,64,64]{4,3,2,1,0:T(8,128)} copy(f32[16,8,5,64,64]{0,1,4,3,2:T(8,128)} %bitcast) | data formatting | bytes 20971520 | tf_op jit(solution)/shard_map/reshape | solution.py:110
  568.4 4.5 reshape.244
  573.1 2.2 gather_fusion.1
  575.2 13.6 %gather.15 = f32[16,8,5,64,8]{4,3,2,1,0:T(8,128)} reshape(f32[640,512]{1,0:T(8,128)S(1)} %gather_fusion.1) | data formatting | bytes 2621440 | tf_op jit(solution)/shard_map/jit(_take)/gather | solution.py:60
  588.8 37.9 %fusion.4 = f32[16,8,5,64,8]{3,4,2,1,0:T(8,128)S(1)} fusion(f32[16,8,5,64,64]{4,3,2,1,0:T(8,128)} %copy.214, f32[16,8,5,64,8]{4,3,2,1,0:T(8,128)} %gather.15, pred[16,8,5]{2,1,0:T(8,128)(4,1)S(1)} %copy.211), kind=kOutput, calls=%fused_computation.16 | convolution fusion | flops 251985920 | bytes 13107840 | tf_op jit(solution)/shard_map/ijkoc,ijkcw->ijkow/dot_general | solution.py:166
  626.7 6.0 copy.215
  632.7 6.8 %copy.216 = f32[16,8,2560]{2,1,0:T(8,128)} copy(f32[16,8,2560]{0,2,1:T(8,128)} %bitcast.84) | data formatting | bytes 2621440
  (112 shorter events, 29.2 us)
Async XLA Ops:
  1.6 61.6 %collective-permute-start.1 = (f32[1,8,2048]{2,0,1:T(1,128)S(1)}, f32[1,8,2048]{2,0,1:T(1,128)S(1)}, u32[]{:S(2)}, u32[]{:S(2)}) collective-permute-start(f32[1,8,2048]{2,0,1:T(1,128)S(1)} %copy.174), channel_id=1, source_target_pairs={{8,0},{16,8},{24,16},{32,24},{40,32},{48,40},{56,48},{64,56},{72,6... | collective-permute-start | bytes 196616 | tf_op jit(solution)/shard_map/ppermute | solution.py:26
  4.1 59.0 %collective-permute-start = (f32[1,8,2048]{2,0,1:T(1,128)S(1)}, f32[1,8,2048]{2,0,1:T(1,128)S(1)}, u32[]{:S(2)}, u32[]{:S(2)}) collective-permute-start(f32[1,8,2048]{2,0,1:T(1,128)S(1)} %copy.173), channel_id=1, source_target_pairs={{0,8},{8,16},{16,24},{24,32},{32,40},{40,48},{48,56},{56,64},{64,7... | collective-permute-start | bytes 196616 | tf_op jit(solution)/shard_map/ppermute | solution.py:24
  11.6 39.3 %copy-start.4 = (s32[16,8,5]{2,1,0:T(8,128)}, s32[16,8,5]{2,1,0:T(8,128)S(1)}, u32[]{:S(2)}) copy-start(s32[16,8,5]{2,1,0:T(8,128)S(1)} %copy.172) | copy-start | bytes 7684
  11.9 39.0 %copy-start.7 = (s32[64]{0:T(128)}, s32[64]{0:T(128)S(1)}, u32[]{:S(2)}) copy-start(s32[64]{0:T(128)S(1)} %and_select_fusion.1) | copy-start | bytes 772
  50.9 11.7 %copy-start.2 = (f32[16,8,2048]{2,1,0:T(8,128)S(1)}, f32[16,8,2048]{2,1,0:T(8,128)}, u32[]{:S(2)}) copy-start(f32[16,8,2048]{2,1,0:T(8,128)} %param.9) | copy-start | bytes 3145732
  63.2 82.5 %collective-permute-start.2 = (f32[18,1,2048]{2,0,1:T(8,128)S(1)}, f32[18,1,2048]{2,0,1:T(8,128)S(1)}, u32[]{:S(2)}, u32[]{:S(2)}) collective-permute-start(f32[18,1,2048]{2,0,1:T(8,128)S(1)} %get-tuple-element.25), channel_id=1, source_target_pairs={{0,1},{1,2},{2,3},{3,4},{4,5},{5,6},{6,7},{8,9},{9,10},{10,11},{11... | collective-permute-start | bytes 442376 | tf_op jit(solution)/shard_map/ppermute | solution.py:24
  67.6 78.2 %collective-permute-start.3 = (f32[18,1,2048]{2,0,1:T(8,128)S(1)}, f32[18,1,2048]{2,0,1:T(8,128)S(1)}, u32[]{:S(2)}, u32[]{:S(2)}) collective-permute-start(f32[18,1,2048]{2,0,1:T(8,128)S(1)} %get-tuple-element.26), channel_id=1, source_target_pairs={{1,0},{2,1},{3,2},{4,3},{5,4},{6,5},{7,6},{9,8},{10,9},{11,10},{12... | collective-permute-start | bytes 442376 | tf_op jit(solution)/shard_map/ppermute | solution.py:26
  211.4 5.2 copy-start
  211.7 12.2 %collective-permute-start.4 = (f32[1,8,2048]{2,1,0:T(8,128)S(1)}, f32[1,8,2048]{2,1,0:T(8,128)S(1)}, u32[]{:S(2)}, u32[]{:S(2)}) collective-permute-start(f32[1,8,2048]{2,1,0:T(8,128)S(1)} %slice.78), channel_id=1, source_target_pairs={{0,8},{8,16},{16,24},{24,32},{32,40},{40,48},{48,56},{56,64},{64,7... | collective-permute-start | bytes 196616 | tf_op jit(solution)/shard_map/ppermute | solution.py:24
  216.8 7.1 %collective-permute-start.5 = (f32[1,8,2048]{2,1,0:T(8,128)S(1)}, f32[1,8,2048]{2,1,0:T(8,128)S(1)}, u32[]{:S(2)}, u32[]{:S(2)}) collective-permute-start(f32[1,8,2048]{2,1,0:T(8,128)S(1)} %slice.80), channel_id=1, source_target_pairs={{8,0},{16,8},{24,16},{32,24},{40,32},{48,40},{56,48},{64,56},{72,6... | collective-permute-start | bytes 196616 | tf_op jit(solution)/shard_map/ppermute | solution.py:26
  224.2 18.0 %collective-permute-start.6 = (f32[18,1,2048]{2,1,0:T(1,128)S(1)}, f32[18,1,2048]{2,1,0:T(1,128)S(1)}, u32[]{:S(2)}, u32[]{:S(2)}) collective-permute-start(f32[18,1,2048]{2,1,0:T(1,128)S(1)} %get-tuple-element.23), channel_id=1, source_target_pairs={{0,1},{1,2},{2,3},{3,4},{4,5},{5,6},{6,7},{8,9},{9,10},{10,11},{11... | collective-permute-start | bytes 442376 | tf_op jit(solution)/shard_map/ppermute | solution.py:24
  228.9 13.2 %collective-permute-start.7 = (f32[18,1,2048]{2,1,0:T(1,128)S(1)}, f32[18,1,2048]{2,1,0:T(1,128)S(1)}, u32[]{:S(2)}, u32[]{:S(2)}) collective-permute-start(f32[18,1,2048]{2,1,0:T(1,128)S(1)} %get-tuple-element.24), channel_id=1, source_target_pairs={{1,0},{2,1},{3,2},{4,3},{5,4},{6,5},{7,6},{9,8},{10,9},{11,10},{12... | collective-permute-start | bytes 442376 | tf_op jit(solution)/shard_map/ppermute | solution.py:26
  231.6 153.6 %all-to-all-start.1 = ((s32[128,1,2]{2,1,0:T(1,128)}), s32[128,1,2]{2,1,0:T(1,128)S(1)}, u32[]{:S(2)}, u32[]{:S(2)}) async-start(s32[128,1,2]{2,1,0:T(1,128)} %copy.196), calls=%async_computation.1 | async-start | bytes 131072 | tf_op jit(solution)/shard_map/all_to_all | solution.py:95
  255.5 13.8 %copy-start.1 = (f32[16,8,64,32]{2,3,1,0:T(8,128)S(1)}, f32[16,8,64,32]{2,3,1,0:T(8,128)}, u32[]{:S(2)}) copy-start(f32[16,8,64,32]{2,3,1,0:T(8,128)} %copy-done) | copy-start | bytes 3145732
  377.6 3.5 copy-start.8
  385.2 35.8 %all-to-all-start = ((f32[128,2,2048]{2,1,0:T(2,128)}), f32[128,2,2048]{2,1,0:T(2,128)S(1)}, u32[]{:S(2)}, u32[]{:S(2)}) async-start(f32[128,2,2048]{2,1,0:T(2,128)} %copy.192), calls=%async_computation | async-start | bytes 4194304 | tf_op jit(solution)/shard_map/all_to_all | solution.py:94
  470.2 13.7 %copy-start.5 = (s32[16,8,5]{2,1,0:T(8,128)S(1)}, s32[16,8,5]{2,1,0:T(8,128)}, u32[]{:S(2)}) copy-start(s32[16,8,5]{2,1,0:T(8,128)} %copy-done.4) | copy-start | bytes 7684
  477.6 18.3 %all-to-all-start.2 = ((f32[128,2,512]{2,1,0:T(2,128)}), f32[128,2,512]{2,1,0:T(2,128)S(1)}, u32[]{:S(2)}, u32[]{:S(2)}) async-start(f32[128,2,512]{2,1,0:T(2,128)} %reshape.249), calls=%async_computation.2 | async-start | bytes 1048576 | tf_op jit(solution)/shard_map/all_to_all | solution.py:101
  496.3 5.8 collective-permute-start.8
  500.1 68.1 %copy-start.3 = (f32[16,8,512]{2,1,0:T(8,128)}, f32[16,8,512]{2,1,0:T(8,128)S(1)}, u32[]{:S(2)}) copy-start(f32[16,8,512]{2,1,0:T(8,128)S(1)} %reshape_reshape_reshape.7) | copy-start | bytes 786436
  500.2 6.6 %collective-permute-start.9 = (f32[1,8,512]{2,1,0:T(8,128)S(1)}, f32[1,8,512]{2,1,0:T(8,128)S(1)}, u32[]{:S(2)}, u32[]{:S(2)}) collective-permute-start(f32[1,8,512]{2,1,0:T(8,128)S(1)} %slice.87), channel_id=1, source_target_pairs={{8,0},{16,8},{24,16},{32,24},{40,32},{48,40},{56,48},{64,56},{72,6... | collective-permute-start | bytes 49160 | tf_op jit(solution)/shard_map/ppermute | solution.py:26
  506.8 66.1 %collective-permute-start.10 = (f32[18,1,512]{2,1,0:T(1,128)S(1)}, f32[18,1,512]{2,1,0:T(1,128)S(1)}, u32[]{:S(2)}, u32[]{:S(2)}) collective-permute-start(f32[18,1,512]{2,1,0:T(1,128)S(1)} %get-tuple-element.29), channel_id=1, source_target_pairs={{0,1},{1,2},{2,3},{3,4},{4,5},{5,6},{6,7},{8,9},{9,10},{10,11},{11... | collective-permute-start | bytes 110600 | tf_op jit(solution)/shard_map/ppermute | solution.py:24
  509.9 63.0 %collective-permute-start.11 = (f32[18,1,512]{2,1,0:T(1,128)S(1)}, f32[18,1,512]{2,1,0:T(1,128)S(1)}, u32[]{:S(2)}, u32[]{:S(2)}) collective-permute-start(f32[18,1,512]{2,1,0:T(1,128)S(1)} %get-tuple-element.30), channel_id=1, source_target_pairs={{1,0},{2,1},{3,2},{4,3},{5,4},{6,5},{7,6},{9,8},{10,9},{11,10},{12... | collective-permute-start | bytes 110600 | tf_op jit(solution)/shard_map/ppermute | solution.py:26
  512.7 55.6 %copy-start.6 = (pred[16,8,5]{0,1,2:T(8,128)(4,1)S(1)}, pred[16,8,5]{0,1,2:T(8,128)(4,1)}, u32[]{:S(2)}) copy-start(pred[16,8,5]{0,1,2:T(8,128)(4,1)} %get-tuple-element.19) | copy-start | bytes 1924
where the time goes:
time: 651 us; the launch traced here: 640 us
  local copies, waits for them, and re-layouts  300 us (46%)
  matrix products  130 us (20%)
  blocking collectives  65.2 us (10%)
  starting transfers between devices  61.2 us (9%)
  waiting for transfers between devices  43.2 us (7%)
  other arithmetic  39.2 us (6%)
    dot_general x2, matrix products, shards(): jnp.einsum('ijor,ijrw->ijow', block_wide, picked, precision=FULL_PRECISION)  76.2 us
    psum x1, blocking collectives, shards(): totals = lax.psum(squares, ('slab', 'pencil'))  65.2 us
    transpose x1, local copies, waits for them, and re-layouts, shards(): jnp.transpose(blocks, (0, 1, 3, 2, 4))  63.1 us
    reshape x1, local copies, waits for them, and re-layouts, shards(): blocks = a_blocks.reshape(height, across_devices, KS, BLK, BLK)  55.6 us
    unnamed x27, local copies, waits for them, and re-layouts  47.3 us
    dot_general x1, matrix products, shards(): jnp.einsum('ijkoc,ijkcw->ijkow', blocks, picked_tiles, precision=FULL_PRE...  37.9 us
    another operation x2, local copies, waits for them, and re-layouts, shards(): pick_rows(padded, flat_index, height, across_devices)  27.5 us
    all_to_all x1, waiting for transfers between devices, send_owner(): lax.all_to_all(payload, ('slab', 'pencil'), split_axis=0, concat_axis=0,...  26.8 us
  transfers between devices with their start and end apart: 15, of which 3 were waited for; matrix products, arithmetic and copies ran while one was open for 43% of the time, Pallas kernels for 0%

commit v1 on v0

--- a/solution.py
+++ b/solution.py
@@ -126,7 +126,7 @@
         image = jnp.einsum("ijor,ijrw->ijow", block_wide, picked, precision=FULL_PRECISION)
         candidate_vectors = candidate_vectors - OMEGA * image / diagonal[:, :, :, None]
     squares = jnp.sum(candidate_vectors * candidate_vectors, axis=(0, 1, 2))
-    totals = lax.psum(squares, ("slab", "pencil"))
+    totals = jnp.sum(lax.all_gather(squares, ("slab", "pencil")), axis=0)
     scale = jnp.sqrt(totals / (height * across_devices * BLK * devices) + 1e-06)
     relaxed = candidate_vectors / scale
     block_rows = height * across_devices

time: 651 us -> 651 us (level)
    psum x1 -> x0, blocking collectives: 65.2 us -> none  [shards(): totals = lax.psum(squares, ('slab', 'pencil'))]
    unnamed x0 -> x1, blocking collectives: none -> 65.2 us
    unnamed x27 -> x29, local copies, waits for them, and re-layouts: 47.3 us -> 47.6 us
where the time goes in v1:
time: 651 us; the launch traced here: 640 us
  local copies, waits for them, and re-layouts  300 us (46%)
  matrix products  130 us (20%)
  blocking collectives  65.2 us (10%)
  starting transfers between devices  61.1 us (9%)
  waiting for transfers between devices  43.2 us (7%)
  other arithmetic  39.3 us (6%)
    dot_general x2, matrix products, shards(): jnp.einsum('ijor,ijrw->ijow', block_wide, picked, precision=FULL_PRECISION)  76.2 us
    unnamed x1, blocking collectives  65.2 us
    transpose x1, local copies, waits for them, and re-layouts, shards(): jnp.transpose(blocks, (0, 1, 3, 2, 4))  63.1 us
    reshape x1, local copies, waits for them, and re-layouts, shards(): blocks = a_blocks.reshape(height, across_devices, KS, BLK, BLK)  55.6 us
    unnamed x29, local copies, waits for them, and re-layouts  47.6 us
    dot_general x1, matrix products, shards(): jnp.einsum('ijkoc,ijkcw->ijkow', blocks, picked_tiles, precision=FULL_PRE...  37.9 us
    another operation x2, local copies, waits for them, and re-layouts, shards(): pick_rows(padded, flat_index, height, across_devices)  27.5 us
    all_to_all x1, waiting for transfers between devices, send_owner(): lax.all_to_all(payload, ('slab', 'pencil'), split_axis=0, concat_axis=0,...  26.8 us
  transfers between devices with their start and end apart: 15, of which 3 were waited for; matrix products, arithmetic and copies ran while one was open for 43% of the time, Pallas kernels for 0%

profile of v1, /device:TPU:7, one launch (start us, length us, event | category | flops | bytes accessed | tf_op | source)
XLA Modules:
  0.0 640.1 jit_solution(8501627585861475378)
XLA Ops:
  1.6 2.5 collective-permute-start.1
  4.1 4.9 collective-permute-start
  11.9 38.9 %copy.177 = f32[16,8,20480]{0,1,2:T(8,128)} copy(f32[16,8,20480]{2,1,0:T(8,128)} %param.6) | data formatting | bytes 20971520 | tf_op args[0]
  50.9 11.6 %slice_bitcast_fusion = f32[16,8,64,64]{0,1,3,2:T(8,128)} fusion(f32[16,8,5,64,64]{0,1,4,3,2:T(8,128)} %bitcast), kind=kLoop, calls=%fused_computation.6 | loop fusion | bytes 4194304 | tf_op jit(solution)/shard_map/squeeze | solution.py:111
  63.2 4.3 collective-permute-start.2
  69.5 2.7 reshape.241
  72.2 3.8 copy.182
  76.0 6.4 %gather_fusion = f32[64,16,8]{1,2,0:T(8,128)S(1)} fusion(f32[16,8,64,64]{0,1,3,2:T(8,128)} %slice_bitcast_fusion, s32[64]{0:T(128)S(1)} %or_bitcast_fusion), kind=kCustom, calls=%fused_computation.2 | custom fusion | bytes 66048 | tf_op jit(solution)/shard_map/jit(diagonal)/gather | solution.py:111
  82.6 63.1 %copy.178 = f32[16,8,64,5,64]{2,4,3,1,0:T(8,128)} copy(f32[16,8,64,5,64]{0,1,4,2,3:T(8,128)} %bitcast.1) | data formatting | bytes 20971520 | tf_op jit(solution)/shard_map/transpose | solution.py:112
  146.1 2.3 copy.176
  150.0 4.6 gather_fusion.2
  154.6 5.2 broadcast_select_fusion.1
  159.8 13.7 %reshape_reshape.7 = f32[16,8,320,32]{3,2,1,0:T(8,128)} reshape(f32[640,2048]{1,0:T(8,128)} %broadcast_select_fusion.1) | data formatting | bytes 10485760 | tf_op jit(solution)/shard_map/reshape;reshape | solution.py:123
  173.5 37.9 %bitcast_subtract_fusion.1 = f32[16,8,64,32]{2,3,1,0:T(8,128)S(1)} fusion(f32[16,8,64,32]{2,3,1,0:T(8,128)} %copy.182, f32[16,8,320,32]{3,2,1,0:T(8,128)} %reshape_reshape.7, f32[16,8,64,320]{2,3,1,0:T(8,128)} %bitcast.82, f32[16,8,64]{2,1,0:T(8,128)S(1)} %copy.181), kind=kOutput, calls=%fused_computation.13 | convolution fusion | flops 1007419392 | bytes 17858560 | tf_op jit(solution)/shard_map/ijor,ijrw->ijow/dot_general | solution.py:126
  213.7 2.8 copy.184
  216.8 3.4 collective-permute-start.5
  220.2 3.6 reshape.246
  224.2 4.7 collective-permute-start.6
  231.6 10.5 %all-to-all-start.1 = ((s32[128,1,2]{2,1,0:T(1,128)}), s32[128,1,2]{2,1,0:T(1,128)S(1)}, u32[]{:S(2)}, u32[]{:S(2)}) async-start(s32[128,1,2]{2,1,0:T(1,128)} %copy.196), calls=%async_computation.1 | async-start | bytes 131072 | tf_op jit(solution)/shard_map/all_to_all | solution.py:95
  245.7 4.6 gather_fusion.3
  250.2 5.2 broadcast_select_fusion
  255.4 13.8 %reshape_reshape.8 = f32[16,8,320,32]{3,2,1,0:T(8,128)} reshape(f32[640,2048]{1,0:T(8,128)} %broadcast_select_fusion) | data formatting | bytes 10485760 | tf_op jit(solution)/shard_map/reshape;reshape | solution.py:123
  269.3 38.3 %multiply_reduce_fusion = (f32[32]{0:T(128)S(1)}, f32[16,8,64,32]{2,3,1,0:T(8,128)}) fusion(f32[16,8,64,32]{2,3,1,0:T(8,128)S(1)} %copy-done.1, f32[16,8,64]{2,1,0:T(8,128)S(1)} %copy.181, f32[16,8,320,32]{3,2,1,0:T(8,128)} %reshape_reshape.8, f32[16,8,64,320]{2,3,1,0:T(8,128)} %bitcast.83), kind=kOutput, calls=%fused_computation.14 | convolution fusion | flops 1007943680 | bytes 17858688 | tf_op jit(solution)/shard_map/ijor,ijrw->ijow/dot_general | solution.py:126
  307.9 65.2 %all-reduce = f32[4096]{0:T(1024)S(1)} all-reduce(f32[4096]{0:T(1024)S(1)} %dynamic-update-slice.3), channel_id=2, replica_groups=mesh['slab'=16,'pencil'=8] {'slab','pencil'}, use_global_device_ids=true, to_apply=%add | all-reduce | flops 4096 | bytes 32768
  375.2 2.8 copy.188
  378.0 3.5 reshape_reshape_reshape.6
  382.6 2.9 copy.192
  385.6 7.2 %all-to-all-start = ((f32[128,2,2048]{2,1,0:T(2,128)}), f32[128,2,2048]{2,1,0:T(2,128)S(1)}, u32[]{:S(2)}, u32[]{:S(2)}) async-start(f32[128,2,2048]{2,1,0:T(2,128)} %copy.192), calls=%async_computation | async-start | bytes 4194304 | tf_op jit(solution)/shard_map/all_to_all | solution.py:94
  394.5 26.8 %all-to-all-done = f32[128,2,2048]{2,1,0:T(2,128)S(1)} async-done(((f32[128,2,2048]{2,1,0:T(2,128)}), f32[128,2,2048]{2,1,0:T(2,128)S(1)}, u32[]{:S(2)}, u32[]{:S(2)}) %all-to-all-start) | async-done | bytes 2097184 | tf_op jit(solution)/shard_map/all_to_all | solution.py:94
  421.3 5.3 reshape.250
  426.6 7.0 %copy.197 = f32[256,64,32]{0,1,2:T(8,128)S(1)} copy(f32[256,64,32]{2,1,0:T(8,128)} %reshape.250) | data formatting | bytes 4194304 | tf_op jit(solution)/shard_map/reshape | solution.py:148
  435.9 11.7 %custom-call.11 = f32[16,8,8]{2,1,0:T(8,128)S(1)} custom-call(f32[16,8,8]{2,1,0:T(8,128)S(1)} %fusion.18), custom_call_target="Cholesky" | custom-call | tf_op jit(solution)/shard_map/jit(cholesky)/cholesky | solution.py:44
  447.9 10.0 %custom-call.12 = f32[16,1,8,8]{2,3,1,0:T(8,128)S(1)} custom-call(f32[16,1,8,8]{3,2,1,0:T(8,128)S(1)} %select_bitcast_fusion), custom_call_target="InvertDiagBlocksLowerTriangular" | custom-call | tf_op jit(solution)/shard_map/jit(_solve_triangular)/vmap()/triangular_solve | solution.py:46
  459.3 11.2 %fusion.56 = f32[256,64,8]{2,1,0:T(8,128)} fusion(f32[256,64,32]{2,1,0:T(8,128)} %reshape.250, f32[256,32,8]{1,2,0:T(8,128)S(1)} %copy.209), kind=kOutput, calls=%fused_computation.114 | convolution fusion | flops 50331648 | bytes 2883584 | tf_op jit(solution)/shard_map/scv,svk->sck/dot_general | solution.py:153
  470.5 7.4 %reshape.253 = f32[128,2,512]{2,1,0:T(2,128)} reshape(f32[256,64,8]{2,1,0:T(8,128)} %fusion.56) | data formatting | bytes 1048576 | tf_op jit(solution)/shard_map/reshape | solution.py:159
  477.8 6.3 all-to-all-start.2
  484.4 11.8 %all-to-all-done.2 = f32[128,2,512]{2,1,0:T(2,128)S(1)} async-done(((f32[128,2,512]{2,1,0:T(2,128)}), f32[128,2,512]{2,1,0:T(2,128)S(1)}, u32[]{:S(2)}, u32[]{:S(2)}) %all-to-all-start.2) | async-done | bytes 524320 | tf_op jit(solution)/shard_map/all_to_all | solution.py:101
  496.6 3.8 collective-permute-start.8
  502.5 4.6 collective-permute-done.9
  507.1 3.1 collective-permute-start.10
  510.2 2.7 collective-permute-start.11
  513.0 55.6 %copy.214 = f32[16,8,5,64,64]{4,3,2,1,0:T(8,128)} copy(f32[16,8,5,64,64]{0,1,4,3,2:T(8,128)} %bitcast) | data formatting | bytes 20971520 | tf_op jit(solution)/shard_map/reshape | solution.py:110
  568.8 4.5 reshape.248
  573.4 2.2 gather_fusion.1
  575.6 13.5 %gather.15 = f32[16,8,5,64,8]{4,3,2,1,0:T(8,128)} reshape(f32[640,512]{1,0:T(8,128)S(1)} %gather_fusion.1) | data formatting | bytes 2621440 | tf_op jit(solution)/shard_map/jit(_take)/gather | solution.py:60
  589.1 37.9 %fusion.4 = f32[16,8,5,64,8]{3,4,2,1,0:T(8,128)S(1)} fusion(f32[16,8,5,64,64]{4,3,2,1,0:T(8,128)} %copy.214, f32[16,8,5,64,8]{4,3,2,1,0:T(8,128)} %gather.15, pred[16,8,5]{2,1,0:T(8,128)(4,1)S(1)} %copy.211), kind=kOutput, calls=%fused_computation.16 | convolution fusion | flops 251985920 | bytes 13107840 | tf_op jit(solution)/shard_map/ijkoc,ijkcw->ijkow/dot_general | solution.py:166
  627.0 6.1 copy.215
  633.1 6.8 %copy.216 = f32[16,8,2560]{2,1,0:T(8,128)} copy(f32[16,8,2560]{0,2,1:T(8,128)} %bitcast.84) | data formatting | bytes 2621440
  (116 shorter events, 29.7 us)
Async XLA Ops:
  1.6 61.6 %collective-permute-start.1 = (f32[1,8,2048]{2,0,1:T(1,128)S(1)}, f32[1,8,2048]{2,0,1:T(1,128)S(1)}, u32[]{:S(2)}, u32[]{:S(2)}) collective-permute-start(f32[1,8,2048]{2,0,1:T(1,128)S(1)} %copy.174), channel_id=1, source_target_pairs={{8,0},{16,8},{24,16},{32,24},{40,32},{48,40},{56,48},{64,56},{72,6... | collective-permute-start | bytes 196616 | tf_op jit(solution)/shard_map/ppermute | solution.py:26
  4.1 59.0 %collective-permute-start = (f32[1,8,2048]{2,0,1:T(1,128)S(1)}, f32[1,8,2048]{2,0,1:T(1,128)S(1)}, u32[]{:S(2)}, u32[]{:S(2)}) collective-permute-start(f32[1,8,2048]{2,0,1:T(1,128)S(1)} %copy.173), channel_id=1, source_target_pairs={{0,8},{8,16},{16,24},{24,32},{32,40},{40,48},{48,56},{56,64},{64,7... | collective-permute-start | bytes 196616 | tf_op jit(solution)/shard_map/ppermute | solution.py:24
  11.6 39.3 %copy-start.4 = (s32[16,8,5]{2,1,0:T(8,128)}, s32[16,8,5]{2,1,0:T(8,128)S(1)}, u32[]{:S(2)}) copy-start(s32[16,8,5]{2,1,0:T(8,128)S(1)} %copy.172) | copy-start | bytes 7684
  11.9 39.0 %copy-start.7 = (s32[64]{0:T(128)}, s32[64]{0:T(128)S(1)}, u32[]{:S(2)}) copy-start(s32[64]{0:T(128)S(1)} %and_select_fusion.1) | copy-start | bytes 772
  50.9 11.7 %copy-start.2 = (f32[16,8,2048]{2,1,0:T(8,128)S(1)}, f32[16,8,2048]{2,1,0:T(8,128)}, u32[]{:S(2)}) copy-start(f32[16,8,2048]{2,1,0:T(8,128)} %param.9) | copy-start | bytes 3145732
  63.2 82.5 %collective-permute-start.2 = (f32[18,1,2048]{2,0,1:T(8,128)S(1)}, f32[18,1,2048]{2,0,1:T(8,128)S(1)}, u32[]{:S(2)}, u32[]{:S(2)}) collective-permute-start(f32[18,1,2048]{2,0,1:T(8,128)S(1)} %get-tuple-element.25), channel_id=1, source_target_pairs={{0,1},{1,2},{2,3},{3,4},{4,5},{5,6},{6,7},{8,9},{9,10},{10,11},{11... | collective-permute-start | bytes 442376 | tf_op jit(solution)/shard_map/ppermute | solution.py:24
  67.6 78.2 %collective-permute-start.3 = (f32[18,1,2048]{2,0,1:T(8,128)S(1)}, f32[18,1,2048]{2,0,1:T(8,128)S(1)}, u32[]{:S(2)}, u32[]{:S(2)}) collective-permute-start(f32[18,1,2048]{2,0,1:T(8,128)S(1)} %get-tuple-element.26), channel_id=1, source_target_pairs={{1,0},{2,1},{3,2},{4,3},{5,4},{6,5},{7,6},{9,8},{10,9},{11,10},{12... | collective-permute-start | bytes 442376 | tf_op jit(solution)/shard_map/ppermute | solution.py:26
  211.4 5.2 copy-start
  211.7 12.2 %collective-permute-start.4 = (f32[1,8,2048]{2,1,0:T(8,128)S(1)}, f32[1,8,2048]{2,1,0:T(8,128)S(1)}, u32[]{:S(2)}, u32[]{:S(2)}) collective-permute-start(f32[1,8,2048]{2,1,0:T(8,128)S(1)} %slice.78), channel_id=1, source_target_pairs={{0,8},{8,16},{16,24},{24,32},{32,40},{40,48},{48,56},{56,64},{64,7... | collective-permute-start | bytes 196616 | tf_op jit(solution)/shard_map/ppermute | solution.py:24
  216.8 7.1 %collective-permute-start.5 = (f32[1,8,2048]{2,1,0:T(8,128)S(1)}, f32[1,8,2048]{2,1,0:T(8,128)S(1)}, u32[]{:S(2)}, u32[]{:S(2)}) collective-permute-start(f32[1,8,2048]{2,1,0:T(8,128)S(1)} %slice.80), channel_id=1, source_target_pairs={{8,0},{16,8},{24,16},{32,24},{40,32},{48,40},{56,48},{64,56},{72,6... | collective-permute-start | bytes 196616 | tf_op jit(solution)/shard_map/ppermute | solution.py:26
  224.2 18.0 %collective-permute-start.6 = (f32[18,1,2048]{2,1,0:T(1,128)S(1)}, f32[18,1,2048]{2,1,0:T(1,128)S(1)}, u32[]{:S(2)}, u32[]{:S(2)}) collective-permute-start(f32[18,1,2048]{2,1,0:T(1,128)S(1)} %get-tuple-element.23), channel_id=1, source_target_pairs={{0,1},{1,2},{2,3},{3,4},{4,5},{5,6},{6,7},{8,9},{9,10},{10,11},{11... | collective-permute-start | bytes 442376 | tf_op jit(solution)/shard_map/ppermute | solution.py:24
  228.9 13.2 %collective-permute-start.7 = (f32[18,1,2048]{2,1,0:T(1,128)S(1)}, f32[18,1,2048]{2,1,0:T(1,128)S(1)}, u32[]{:S(2)}, u32[]{:S(2)}) collective-permute-start(f32[18,1,2048]{2,1,0:T(1,128)S(1)} %get-tuple-element.24), channel_id=1, source_target_pairs={{1,0},{2,1},{3,2},{4,3},{5,4},{6,5},{7,6},{9,8},{10,9},{11,10},{12... | collective-permute-start | bytes 442376 | tf_op jit(solution)/shard_map/ppermute | solution.py:26
  231.6 154.0 %all-to-all-start.1 = ((s32[128,1,2]{2,1,0:T(1,128)}), s32[128,1,2]{2,1,0:T(1,128)S(1)}, u32[]{:S(2)}, u32[]{:S(2)}) async-start(s32[128,1,2]{2,1,0:T(1,128)} %copy.196), calls=%async_computation.1 | async-start | bytes 131072 | tf_op jit(solution)/shard_map/all_to_all | solution.py:95
  255.4 13.8 %copy-start.1 = (f32[16,8,64,32]{2,3,1,0:T(8,128)S(1)}, f32[16,8,64,32]{2,3,1,0:T(8,128)}, u32[]{:S(2)}) copy-start(f32[16,8,64,32]{2,3,1,0:T(8,128)} %copy-done) | copy-start | bytes 3145732
  378.0 3.5 copy-start.8
  385.6 35.7 %all-to-all-start = ((f32[128,2,2048]{2,1,0:T(2,128)}), f32[128,2,2048]{2,1,0:T(2,128)S(1)}, u32[]{:S(2)}, u32[]{:S(2)}) async-start(f32[128,2,2048]{2,1,0:T(2,128)} %copy.192), calls=%async_computation | async-start | bytes 4194304 | tf_op jit(solution)/shard_map/all_to_all | solution.py:94
  470.5 13.7 %copy-start.5 = (s32[16,8,5]{2,1,0:T(8,128)S(1)}, s32[16,8,5]{2,1,0:T(8,128)}, u32[]{:S(2)}) copy-start(s32[16,8,5]{2,1,0:T(8,128)} %copy-done.4) | copy-start | bytes 7684
  477.8 18.3 %all-to-all-start.2 = ((f32[128,2,512]{2,1,0:T(2,128)}), f32[128,2,512]{2,1,0:T(2,128)S(1)}, u32[]{:S(2)}, u32[]{:S(2)}) async-start(f32[128,2,512]{2,1,0:T(2,128)} %reshape.253), calls=%async_computation.2 | async-start | bytes 1048576 | tf_op jit(solution)/shard_map/all_to_all | solution.py:101
  496.6 5.8 collective-permute-start.8
  500.4 68.2 %copy-start.3 = (f32[16,8,512]{2,1,0:T(8,128)}, f32[16,8,512]{2,1,0:T(8,128)S(1)}, u32[]{:S(2)}) copy-start(f32[16,8,512]{2,1,0:T(8,128)S(1)} %reshape_reshape_reshape.7) | copy-start | bytes 786436
  500.5 6.6 %collective-permute-start.9 = (f32[1,8,512]{2,1,0:T(8,128)S(1)}, f32[1,8,512]{2,1,0:T(8,128)S(1)}, u32[]{:S(2)}, u32[]{:S(2)}) collective-permute-start(f32[1,8,512]{2,1,0:T(8,128)S(1)} %slice.87), channel_id=1, source_target_pairs={{8,0},{16,8},{24,16},{32,24},{40,32},{48,40},{56,48},{64,56},{72,6... | collective-permute-start | bytes 49160 | tf_op jit(solution)/shard_map/ppermute | solution.py:26
  507.1 66.1 %collective-permute-start.10 = (f32[18,1,512]{2,1,0:T(1,128)S(1)}, f32[18,1,512]{2,1,0:T(1,128)S(1)}, u32[]{:S(2)}, u32[]{:S(2)}) collective-permute-start(f32[18,1,512]{2,1,0:T(1,128)S(1)} %get-tuple-element.29), channel_id=1, source_target_pairs={{0,1},{1,2},{2,3},{3,4},{4,5},{5,6},{6,7},{8,9},{9,10},{10,11},{11... | collective-permute-start | bytes 110600 | tf_op jit(solution)/shard_map/ppermute | solution.py:24
  510.2 63.0 %collective-permute-start.11 = (f32[18,1,512]{2,1,0:T(1,128)S(1)}, f32[18,1,512]{2,1,0:T(1,128)S(1)}, u32[]{:S(2)}, u32[]{:S(2)}) collective-permute-start(f32[18,1,512]{2,1,0:T(1,128)S(1)} %get-tuple-element.30), channel_id=1, source_target_pairs={{1,0},{2,1},{3,2},{4,3},{5,4},{6,5},{7,6},{9,8},{10,9},{11,10},{12... | collective-permute-start | bytes 110600 | tf_op jit(solution)/shard_map/ppermute | solution.py:26
  513.0 55.6 %copy-start.6 = (pred[16,8,5]{0,1,2:T(8,128)(4,1)S(1)}, pred[16,8,5]{0,1,2:T(8,128)(4,1)}, u32[]{:S(2)}) copy-start(pred[16,8,5]{0,1,2:T(8,128)(4,1)} %get-tuple-element.19) | copy-start | bytes 1924
